TPU v7x, 32 devices: a whole 2x2x4 slice. The times are simulated.
32 devices in a mesh: tensor: 2 (over y), context: 16 (over z, x, core).
Axes of the slice: x: 2, y: 2, z: 4, core: 2. Of those that a mesh axis runs over, the one named last changes fastest.
Arguments:
- query_stream: bfloat16 [8192, 2048], P('tensor', 'context'), may hold values from -6 to 6
- key_stream: bfloat16 [8192, 2048], P('tensor', 'context'), may hold values from -6 to 6
- value_stream: bfloat16 [8192, 2048], P('tensor', 'context'), may hold values from -6 to 6
- filter_taps: bfloat16 [2048, 8192], P(('tensor', 'context')), may hold values from -0.125 to 0.125
- short_filters: float32 [3, 3, 8192], P(None, None, ('tensor', 'context')), may hold values from -3 to 3
- skip_gain: float32 [8192], P(('tensor', 'context')), may hold values from 0.5 to 1.5
Outputs:
- gated_out: bfloat16 [8192, 2048], P('tensor', 'context')
All inputs are finite; a program needn't handle non-finite values.
Results may differ from a plain program's by a relative error of at most 0.0057.
Values may be sent and summed in bfloat16 or wider, within the bound.
A program may use at most 128 MiB of HBM per device.

v0:
```python
import math
import jax
import jax.numpy as jnp
from jax import lax
from jax.sharding import PartitionSpec as P

HIGHEST = lax.Precision.HIGHEST
THREEPASS = lax.Precision.HIGH
first_order = 128


def shifted(value, axis, steps):
    count = lax.axis_size(axis)
    initial, last = (max(0, -steps), min(count, count - steps))
    return lax.ppermute(value, axis, [(source, source + steps) for source in range(initial, last)])


def unit_tables(size_left, size_right, modulus):
    index_left = jnp.arange(size_left, dtype=jnp.int32)
    index_right = jnp.arange(size_right, dtype=jnp.int32)
    phases = (index_left[:, None] * index_right[None, :] % modulus).astype(jnp.float32)
    radians = phases * (2.0 * math.pi / modulus)
    return (jnp.cos(radians), -jnp.sin(radians))


def short_filter(signal, weights, before):
    joined = jnp.concatenate([before, signal], axis=1)
    length = signal.shape[1]
    return (
        weights[0][:, None] * joined[:, 2:]
        + weights[1][:, None] * joined[:, 1 : length + 1]
        + weights[2][:, None] * joined[:, :length]
    )


def causal_mix(inputs, filters):
    channels, length = inputs.shape
    modulus = 2 * length
    second = modulus // first_order
    half_rows = first_order // 2
    first_cos, first_sin = unit_tables(first_order, first_order, first_order)
    second_cos, second_sin = unit_tables(second, second, second)
    twist_cos, twist_sin = unit_tables(first_order, second, modulus)
    head_cos = first_cos[:, :half_rows]
    head_sin = first_sin[:, :half_rows]

    def forward(signal):
        shaped = signal.reshape(channels, half_rows, second)
        part_real = jnp.einsum("kn,cnm->ckm", head_cos, shaped, precision=THREEPASS)
        part_imag = jnp.einsum("kn,cnm->ckm", head_sin, shaped, precision=THREEPASS)
        turn_real = part_real * twist_cos - part_imag * twist_sin
        turn_imag = part_real * twist_sin + part_imag * twist_cos
        out_real = jnp.einsum("ckm,mj->ckj", turn_real, second_cos, precision=HIGHEST) - jnp.einsum(
            "ckm,mj->ckj", turn_imag, second_sin, precision=HIGHEST
        )
        out_imag = jnp.einsum("ckm,mj->ckj", turn_real, second_sin, precision=HIGHEST) + jnp.einsum(
            "ckm,mj->ckj", turn_imag, second_cos, precision=HIGHEST
        )
        return (out_real, out_imag)

    input_real, input_imag = forward(inputs)
    filter_real, filter_imag = forward(filters)
    product_real = input_real * filter_real - input_imag * filter_imag
    product_imag = input_real * filter_imag + input_imag * filter_real
    back_real = jnp.einsum("ckm,mj->ckj", product_real, second_cos, precision=HIGHEST) + jnp.einsum(
        "ckm,mj->ckj", product_imag, second_sin, precision=HIGHEST
    )
    back_imag = jnp.einsum("ckm,mj->ckj", product_imag, second_cos, precision=HIGHEST) - jnp.einsum(
        "ckm,mj->ckj", product_real, second_sin, precision=HIGHEST
    )
    untwist_real = back_real * twist_cos + back_imag * twist_sin
    untwist_imag = back_imag * twist_cos - back_real * twist_sin
    result = jnp.einsum(
        "nk,ckm->cnm", first_cos[:half_rows, :], untwist_real, precision=HIGHEST
    ) + jnp.einsum("nk,ckm->cnm", first_sin[:half_rows, :], untwist_imag, precision=HIGHEST)
    return (result / modulus).reshape(channels, length)


def local(query_stream, key_stream, value_stream, filter_taps, short_filters, skip_gain):
    group_width, block_rows = query_stream.shape
    context_size = lax.axis_size("context")
    tensor_size = lax.axis_size("tensor")
    local_channels = group_width // context_size
    offset_rows = filter_taps.shape[0]
    laid_out = filter_taps.reshape(offset_rows, tensor_size, context_size, local_channels)
    arrived_taps = lax.all_to_all(laid_out, "tensor", split_axis=1, concat_axis=0, tiled=True)
    arrived_taps = lax.all_to_all(arrived_taps, "context", split_axis=2, concat_axis=0, tiled=True)
    filters = arrived_taps.reshape(context_size, tensor_size, offset_rows, local_channels)
    filters = filters.transpose(3, 1, 0, 2).reshape(local_channels, -1)
    filters = filters.astype(jnp.float32)
    weights = lax.all_gather(short_filters, "context", axis=2, tiled=True)
    rim_cols = shifted(jnp.stack([query_stream, key_stream, value_stream])[:, :, -2:], "context", 1)
    rim_cols = rim_cols.astype(jnp.float32)
    query_short = short_filter(query_stream.astype(jnp.float32), weights[0], rim_cols[0])
    key_short = short_filter(key_stream.astype(jnp.float32), weights[1], rim_cols[1])
    value_short = short_filter(value_stream.astype(jnp.float32), weights[2], rim_cols[2])
    products = (key_short * value_short).astype(jnp.bfloat16)
    arrived = lax.all_to_all(
        products.reshape(context_size, local_channels, block_rows),
        "context",
        split_axis=0,
        concat_axis=2,
        tiled=True,
    )
    arrived = arrived[0].astype(jnp.float32)
    convolved = causal_mix(arrived, filters)
    mixed_out = (convolved + skip_gain[:, None] * arrived).astype(jnp.bfloat16)
    returned = lax.all_to_all(mixed_out[None], "context", split_axis=2, concat_axis=0, tiled=True)
    returned = returned.reshape(group_width, block_rows)
    return (query_short * returned.astype(jnp.float32)).astype(jnp.bfloat16)


def solution(mesh):
    placed = (
        P("tensor", "context"),
        P("tensor", "context"),
        P("tensor", "context"),
        P(("tensor", "context"), None),
        P(None, None, ("tensor", "context")),
        P(("tensor", "context")),
    )
    return jax.shard_map(
        local, mesh=mesh, in_specs=placed, out_specs=P("tensor", "context"), check_vma=False
    )
```

profile of v0, /device:TPU:13, one launch (start us, length us, event | category | flops | bytes accessed | tf_op | source)
XLA Modules:
  0.0 307.0 jit_solution(17208289329332975849)
XLA Ops:
  16.3 18.4 %all_gather.3 = f32[3,3,4096]{2,1,0:T(4,128)S(1)} all-gather(f32[3,3,256]{2,1,0:T(4,128)S(1)} %copy-done.12), channel_id=1, replica_groups=mesh['tensor'=2,'context'=16] {'context'}, dimensions={2}, use_global_device_ids=true | all-gather | bytes 156672 | tf_op jit(solution)/shard_map/all_gather | solution.py:91
  42.7 7.9 %fusion.29 = bf16[4096,128]{1,0:T(8,128)(2,1)} fusion(f32[4096,2]{1,0:T(8,128)S(1)} %get-tuple-element.12, f32[4096,128]{1,0:T(8,128)S(1)} %copy-done.8, f32[4096,2]{1,0:T(8,128)S(1)} %get-tuple-element.11, f32[4096,128]{1,0:T(8,128)S(1)} %copy-done.7, f32[4096]{0:T(1024)S(1)} %bitcast.149, f32[4096]{0:T(1024)S(1)} %bitcast.150, f32[4096]{0:T(1024)S(1)} %bitcast.151, ...), kind=kLoop, calls=%fused_computation.43 | loop fusion | flops 8388608 | bytes 5406720 | tf_op jit(solution)/shard_map/convert_element_type | solution.py:97
  50.6 6.5 %all-to-all-start = ((bf16[16,256,128]{2,1,0:T(8,128)(2,1)}), bf16[16,256,128]{2,1,0:T(8,128)(2,1)S(1)}, u32[]{:S(2)}, u32[]{:S(2)}) async-start(bf16[16,256,128]{2,1,0:T(8,128)(2,1)} %bitcast.15), calls=%async_computation | async-start | bytes 2097152 | tf_op jit(solution)/shard_map/all_to_all | solution.py:98
  60.3 21.7 %all-to-all-done = bf16[16,256,128]{2,1,0:T(8,128)(2,1)S(1)} async-done(((bf16[16,256,128]{2,1,0:T(8,128)(2,1)}), bf16[16,256,128]{2,1,0:T(8,128)(2,1)S(1)}, u32[]{:S(2)}, u32[]{:S(2)}) %all-to-all-start) | async-done | bytes 1048608 | tf_op jit(solution)/shard_map/all_to_all | solution.py:98
  82.0 5.3 %all-to-all-start.2 = ((bf16[128,1,16,256]{3,0,1,2:T(8,128)(2,1)}), bf16[128,1,16,256]{3,0,1,2:T(8,128)(2,1)S(1)}, u32[]{:S(2)}, u32[]{:S(2)}) async-start(bf16[128,1,16,256]{3,0,1,2:T(8,128)(2,1)} %copy.105), calls=%async_computation.2 | async-start | bytes 2097152 | tf_op jit(solution)/shard_map/all_to_all | solution.py:87
  96.7 6.4 %fusion.12 = f32[256,128,32]{1,2,0:T(8,128)S(1)} fusion(f32[256,128,32]{1,0,2:T(8,128)S(1)} %get-tuple-element.10), kind=kOutput, calls=%fused_computation.28 | convolution fusion | flops 402668544 | bytes 8388608 | tf_op jit(solution)/shard_map/ckm,mj->ckj/dot_general | solution.py:53
  103.1 9.1 %fusion.10 = f32[256,128,32]{1,2,0:T(8,128)} fusion(f32[256,128,32]{1,0,2:T(8,128)S(1)} %get-tuple-element.10), kind=kOutput, calls=%fused_computation.26 | convolution fusion | flops 402667520 | bytes 8388608 | tf_op jit(solution)/shard_map/ckm,mj->ckj/dot_general | solution.py:56
  112.1 8.9 %fusion.18 = f32[256,128,32]{1,2,0:T(8,128)} fusion(f32[256,128,32]{1,2,0:T(8,128)S(1)} %fusion.12, f32[256,128,32]{1,0,2:T(8,128)S(1)} %get-tuple-element.9), kind=kOutput, calls=%fused_computation.34 | convolution fusion | flops 403716096 | bytes 12582912 | tf_op jit(solution)/shard_map/ckm,mj->ckj/dot_general | solution.py:53
  122.7 5.7 %add_bitcast_fusion = (f32[256,128,32]{0,1,2:T(8,128)}, f32[256,128,32]{0,1,2:T(8,128)}) fusion(f32[128,256,32]{1,0,2:T(8,128)S(1)} %fusion.51, f32[128,32]{0,1:T(8,128)S(1)} %get-tuple-element.23, f32[128,32]{0,1:T(8,128)S(1)} %get-tuple-element.24, bf16[256,64,32]{0,2,1:T(8,128)(2,1)S(1)} %bitcast.136, f32[128,128]{0,1:T(8,128)S(1)} %fusion.65), kind=kOutput, calls=%fused_computation.24 | convolution fusion | flops 408944640 | bytes 13697024 | tf_op jit(solution)/shard_map/kn,cnm->ckm/dot_general | solution.py:49
  128.3 5.8 %copy.109 = f32[256,128,32]{1,2,0:T(8,128)} copy(f32[256,128,32]{0,1,2:T(8,128)} %get-tuple-element.8) | data formatting | bytes 8388608 | tf_op jit(solution)/shard_map/sub | solution.py:51
  134.2 8.0 %fusion.76 = f32[256,128,32]{1,2,0:T(8,128)} fusion(f32[256,128,32]{1,2,0:T(8,128)} %copy.109), kind=kOutput, calls=%fused_computation.113 | convolution fusion | flops 402668544 | bytes 8388608 | tf_op jit(solution)/shard_map/ckm,mj->ckj/dot_general | solution.py:56
  142.2 5.4 %fusion.87 = f32[256,128,32]{1,2,0:T(8,128)} fusion(f32[256,128,32]{1,2,0:T(8,128)S(1)} %copy-done.3), kind=kOutput, calls=%fused_computation.124 | convolution fusion | flops 402667520 | bytes 8388608 | tf_op jit(solution)/shard_map/ckm,mj->ckj/dot_general | solution.py:53
  147.5 5.5 %copy.110 = f32[256,128,32]{1,2,0:T(8,128)} copy(f32[256,128,32]{0,1,2:T(8,128)} %get-tuple-element.7) | data formatting | bytes 8388608 | tf_op jit(solution)/shard_map/add | solution.py:52
  153.0 7.7 %convolution_add_fusion = f32[256,128,32]{1,2,0:T(8,128)S(1)} fusion(f32[256,128,32]{1,2,0:T(8,128)} %fusion.76, f32[256,128,32]{1,2,0:T(8,128)} %copy.110), kind=kOutput, calls=%fused_computation.36 | convolution fusion | flops 403716096 | bytes 12582912 | tf_op jit(solution)/shard_map/ckm,mj->ckj/dot_general | solution.py:56
  160.8 5.3 %convolution_subtract_fusion = f32[256,128,32]{1,2,0:T(8,128)} fusion(f32[256,128,32]{1,2,0:T(8,128)S(1)} %copy-done.5, f32[256,128,32]{1,2,0:T(8,128)S(1)} %copy-done.2), kind=kOutput, calls=%fused_computation.37 | convolution fusion | flops 403717120 | bytes 12582912 | tf_op jit(solution)/shard_map/ckm,mj->ckj/dot_general | solution.py:53
  166.1 11.6 %multiply_subtract_fusion = (f32[256,128,32]{1,2,0:T(8,128)S(1)}, f32[256,128,32]{1,2,0:T(8,128)S(1)}) fusion(f32[256,128,32]{1,2,0:T(8,128)S(1)} %convolution_add_fusion, f32[256,128,32]{1,2,0:T(8,128)S(1)} %copy-done.4, f32[256,128,32]{1,2,0:T(8,128)} %convolution_subtract_fusion, f32[256,128,32]{1,2,0:T(8,128)} %fusion.10, f32[256,128,32]{1,0,2:T(8,128)S(1)} %copy-done.1), kind=kOutput, calls=%fused_computation.23 | convolution fusion | flops 410008576 | bytes 29360128 | tf_op jit(solution)/shard_map/ckm,mj->ckj/dot_general | solution.py:56
  194.1 17.6 %fusion.2 = f32[256,32,64]{0,2,1:T(8,128)S(1)} fusion(f32[128,32]{0,1:T(8,128)S(1)} %get-tuple-element.23, f32[128,32]{0,1:T(8,128)S(1)} %get-tuple-element.24, f32[256,128,32]{1,2,0:T(8,128)S(1)} %fusion.74, f32[256,128,32]{1,2,0:T(8,128)S(1)} %fusion.83, f32[256,128,32]{1,2,0:T(8,128)S(1)} %fusion.72, f32[256,128,32]{1,2,0:T(8,128)S(1)} %fusion.81, ...), kind=kOutput, calls=%fused_computation.14 | convolution fusion | flops 810549248 | bytes 18972672 | tf_op jit(solution)/shard_map/nk,ckm->cnm/dot_general | solution.py:75
  211.8 17.6 %multiply_bitcast_fusion = f32[256,64,32]{0,1,2:T(8,128)S(1)} fusion(f32[256,32,64]{0,2,1:T(8,128)S(1)} %fusion.2, f32[128,32]{0,1:T(8,128)S(1)} %get-tuple-element.23, f32[128,32]{0,1:T(8,128)S(1)} %get-tuple-element.24, f32[256,128,32]{1,2,0:T(8,128)S(1)} %fusion.74, f32[256,128,32]{1,2,0:T(8,128)S(1)} %fusion.83, f32[256,128,32]{1,2,0:T(8,128)S(1)} %fusion.72, ...), kind=kOutput, calls=%fused_computation.67 | convolution fusion | flops 811597824 | bytes 21069824 | tf_op jit(solution)/shard_map/nk,ckm->cnm/dot_general | solution.py:73
  231.4 11.7 %copy.186 = bf16[1,256,2048]{1,0,2:T(2,128)(2,1)S(1)} copy(bf16[1,256,2048]{1,2,0:T(8,128)(2,1)S(1)} %fusion.44) | data formatting | bytes 2097152 | tf_op jit(solution)/shard_map/convert_element_type | solution.py:107
  243.7 11.5 %reduce = bf16[2048,256]{1,0:T(8,128)(2,1)} reduce(bf16[2048,1,256]{2,1,0:T(2,128)(2,1)S(1)} %bitcast.138, bf16[]{:T(256)} %broadcast.146), dimensions={1}, to_apply=%bitcast.131.reduce_sub_computation | reduce | bytes 2097154
  257.3 6.0 %all-to-all-start.3 = ((bf16[16,2,16384]{2,1,0:T(2,128)(2,1)}), bf16[16,2,16384]{2,1,0:T(2,128)(2,1)}, u32[]{:S(2)}, u32[]{:S(2)}) async-start(bf16[16,2,16384]{2,1,0:T(2,128)(2,1)} %reshape.154), calls=%async_computation.3 | async-start | bytes 2097152 | tf_op jit(solution)/shard_map/all_to_all | solution.py:108
  263.5 24.9 %all-to-all-done.3 = bf16[16,2,16384]{2,1,0:T(2,128)(2,1)} async-done(((bf16[16,2,16384]{2,1,0:T(2,128)(2,1)}), bf16[16,2,16384]{2,1,0:T(2,128)(2,1)}, u32[]{:S(2)}, u32[]{:S(2)}) %all-to-all-start.3) | async-done | bytes 1048608 | tf_op jit(solution)/shard_map/all_to_all | solution.py:108
  288.4 5.8 %reshape.155 = bf16[2048,1,256]{2,1,0:T(2,128)(2,1)} reshape(bf16[16,2,16384]{2,1,0:T(2,128)(2,1)} %all-to-all-done.3) | data formatting | bytes 2097152
  300.3 6.4 %fusion.39 = bf16[4096,128]{1,0:T(8,128)(2,1)} fusion(f32[4096,2]{1,0:T(8,128)} %get-tuple-element.13, f32[4096,128]{1,0:T(8,128)S(1)} %convert_element_type.124, f32[16,1,256,128]{3,2,0,1:T(8,128)} %copy.125, f32[4096]{0:T(1024)S(1)} %bitcast.147, f32[4096]{0:T(1024)S(1)} %bitcast.148, f32[4096]{0:T(1024)S(1)} %bitcast.146), kind=kLoop, calls=%fused_computation.53 | loop fusion | flops 4718592 | bytes 5324800 | tf_op jit(solution)/shard_map/convert_element_type | solution.py:110
  (68 shorter events, 65.8 us)
Async XLA Ops:
  0.0 3.1 %copy-start.10 = (bf16[4096,128]{1,0:T(8,128)(2,1)S(1)}, bf16[4096,128]{1,0:T(8,128)(2,1)}, u32[]{:S(2)}) copy-start(bf16[4096,128]{1,0:T(8,128)(2,1)} %param.8) | copy-start | bytes 3145732
  4.4 11.9 %copy-start.12 = (f32[3,3,256]{2,1,0:T(4,128)S(1)}, f32[3,3,256]{2,1,0:T(4,128)}, u32[]{:S(2)}) copy-start(f32[3,3,256]{2,1,0:T(4,128)} %param.10) | copy-start | bytes 27652
  5.3 29.5 %copy-start.9 = (bf16[4096,128]{1,0:T(8,128)(2,1)S(1)}, bf16[4096,128]{1,0:T(8,128)(2,1)}, u32[]{:S(2)}) copy-start(bf16[4096,128]{1,0:T(8,128)(2,1)} %param.7) | copy-start | bytes 3145732
  5.3 32.4 %collective-permute-start = (bf16[3,4096,2]{1,2,0:T(2,128)(2,1)S(1)}, bf16[3,4096,2]{1,2,0:T(2,128)(2,1)S(1)}, u32[]{:S(2)}, u32[]{:S(2)}) collective-permute-start(bf16[3,4096,2]{1,2,0:T(2,128)(2,1)S(1)} %pad_maximum_fusion.3), channel_id=1, source_target_pairs={{0,1},{1,2},{2,3},{3,4},{4,5},{5,6},{6,7},{7,8},{8,9},{9,10},{10,1... | collective-permute-start | bytes 147464 | tf_op jit(solution)/shard_map/ppermute | solution.py:15
  11.7 38.9 %all-to-all-start.1 = ((bf16[64,2,16,256]{3,2,0,1:T(8,128)(2,1)}), bf16[64,2,16,256]{3,2,0,1:T(8,128)(2,1)}, u32[]{:S(2)}, u32[]{:S(2)}) async-start(bf16[64,2,16,256]{3,2,0,1:T(8,128)(2,1)} %copy.104), calls=%async_computation.1 | async-start | bytes 2097152 | tf_op jit(solution)/shard_map/all_to_all | solution.py:86
  39.7 2.1 copy-start.7
  39.7 3.0 copy-start.8
  50.6 31.5 %all-to-all-start = ((bf16[16,256,128]{2,1,0:T(8,128)(2,1)}), bf16[16,256,128]{2,1,0:T(8,128)(2,1)S(1)}, u32[]{:S(2)}, u32[]{:S(2)}) async-start(bf16[16,256,128]{2,1,0:T(8,128)(2,1)} %bitcast.15), calls=%async_computation | async-start | bytes 2097152 | tf_op jit(solution)/shard_map/all_to_all | solution.py:98
  82.0 39.0 %all-to-all-start.2 = ((bf16[128,1,16,256]{3,0,1,2:T(8,128)(2,1)}), bf16[128,1,16,256]{3,0,1,2:T(8,128)(2,1)S(1)}, u32[]{:S(2)}, u32[]{:S(2)}) async-start(bf16[128,1,16,256]{3,0,1,2:T(8,128)(2,1)} %copy.105), calls=%async_computation.2 | async-start | bytes 2097152 | tf_op jit(solution)/shard_map/all_to_all | solution.py:87
  96.7 15.4 %copy-start = (f32[256,128,32]{1,0,2:T(8,128)}, f32[256,128,32]{1,0,2:T(8,128)S(1)}, u32[]{:S(2)}) copy-start(f32[256,128,32]{1,0,2:T(8,128)S(1)} %get-tuple-element.9) | copy-start | bytes 12582916
  134.2 8.0 %copy-start.3 = (f32[256,128,32]{1,2,0:T(8,128)S(1)}, f32[256,128,32]{1,2,0:T(8,128)}, u32[]{:S(2)}) copy-start(f32[256,128,32]{1,2,0:T(8,128)} %copy.109) | copy-start | bytes 12582916
  153.0 7.7 %copy-start.2 = (f32[256,128,32]{1,2,0:T(8,128)S(1)}, f32[256,128,32]{1,2,0:T(8,128)}, u32[]{:S(2)}) copy-start(f32[256,128,32]{1,2,0:T(8,128)} %copy.110) | copy-start | bytes 12582916
  153.0 7.7 %copy-start.5 = (f32[256,128,32]{1,2,0:T(8,128)S(1)}, f32[256,128,32]{1,2,0:T(8,128)}, u32[]{:S(2)}) copy-start(f32[256,128,32]{1,2,0:T(8,128)} %fusion.87) | copy-start | bytes 12582916
  160.7 5.3 %copy-start.1 = (f32[256,128,32]{1,0,2:T(8,128)S(1)}, f32[256,128,32]{1,0,2:T(8,128)}, u32[]{:S(2)}) copy-start(f32[256,128,32]{1,0,2:T(8,128)} %copy-done) | copy-start | bytes 12582916
  160.8 5.3 %copy-start.4 = (f32[256,128,32]{1,2,0:T(8,128)S(1)}, f32[256,128,32]{1,2,0:T(8,128)}, u32[]{:S(2)}) copy-start(f32[256,128,32]{1,2,0:T(8,128)} %fusion.18) | copy-start | bytes 12582916
  229.4 1.6 copy-start.6
  229.4 1.6 copy-start.13
  243.1 20.2 %copy-start.11 = (bf16[4096,128]{1,0:T(8,128)(2,1)S(1)}, bf16[4096,128]{1,0:T(8,128)(2,1)}, u32[]{:S(2)}) copy-start(bf16[4096,128]{1,0:T(8,128)(2,1)} %param.6) | copy-start | bytes 3145732
  257.3 31.0 %all-to-all-start.3 = ((bf16[16,2,16384]{2,1,0:T(2,128)(2,1)}), bf16[16,2,16384]{2,1,0:T(2,128)(2,1)}, u32[]{:S(2)}, u32[]{:S(2)}) async-start(bf16[16,2,16384]{2,1,0:T(2,128)(2,1)} %reshape.154), calls=%async_computation.3 | async-start | bytes 2097152 | tf_op jit(solution)/shard_map/all_to_all | solution.py:108
where the time goes:
time: 312 us; the launch traced here: 307 us
  matrix products  125 us (40%)
  local copies, waits for them, and re-layouts  55.5 us (18%)
  waiting for transfers between devices  46.6 us (15%)
  other arithmetic  34.2 us (11%)
  starting transfers between devices  26.3 us (8%)
  blocking collectives  18.4 us (6%)
    all_to_all x1, waiting for transfers between devices, local(): lax.all_to_all(mixed_out[None], 'context', split_axis=2, concat_axis=0, t...  24.9 us
    all_to_all x1, waiting for transfers between devices, local(): lax.all_to_all(products.reshape(context_size, local_channels, block_rows)...  21.7 us
    dot_general x2, matrix products, forward(): jnp.einsum('ckm,mj->ckj', turn_real, second_sin, precision=HIGHEST)  19.6 us
    all_gather x1, blocking collectives, local(): weights = lax.all_gather(short_filters, 'context', axis=2, tiled=True)  18.4 us
    dot_general x1, matrix products, causal_mix(): jnp.einsum('nk,ckm->cnm', first_cos[:half_rows, :], untwist_real, precisi...  17.6 us
    dot_general x1, matrix products, causal_mix(): jnp.einsum('nk,ckm->cnm', first_sin[:half_rows, :], untwist_imag, precisi...  17.6 us
    dot_general x2, matrix products, forward(): jnp.einsum('ckm,mj->ckj', turn_imag, second_cos, precision=HIGHEST)  16.8 us
    unnamed x35, local copies, waits for them, and re-layouts  16 us
  transfers between devices with their start and end apart: 5, of which 2 were waited for; matrix products, arithmetic and copies ran while one was open for 18% of the time, Pallas kernels for 0%

commit v1 on v0

--- a/solution.py
+++ b/solution.py
@@ -105,7 +105,10 @@
     arrived = arrived[0].astype(jnp.float32)
     convolved = causal_mix(arrived, filters)
     mixed_out = (convolved + skip_gain[:, None] * arrived).astype(jnp.bfloat16)
-    returned = lax.all_to_all(mixed_out[None], "context", split_axis=2, concat_axis=0, tiled=True)
+    part = mixed_out[None]
+    pieces = jnp.split(part, lax.axis_size("context"), axis=2)
+    received = lax.all_to_all(jnp.stack(pieces), "context", 0, 0)
+    returned = jnp.concatenate(received, axis=0)
     returned = returned.reshape(group_width, block_rows)
     return (query_short * returned.astype(jnp.float32)).astype(jnp.bfloat16)
 

time: 312 us -> 287 us (0.920)
  other arithmetic: 34.2 us -> 21.3 us
  local copies, waits for them, and re-layouts: 55.5 us -> 43.1 us
    convert_element_type x1 -> x0, local copies, waits for them, and re-layouts: 11.7 us -> none  [local(): mixed_out = (convolved + skip_gain[:, None] * arrived).astype(jnp.bfloat16)]
    unnamed x1 -> x0, other arithmetic: 11.5 us -> none
    convert_element_type x2 -> x1, other arithmetic: 7.96 us -> 6.5 us  [local(): return (query_short * returned.astype(jnp.float32)).astype(jnp.bfloat16)]
    unnamed x35 -> x47, local copies, waits for them, and re-layouts: 16 us -> 17 us
  transfers between devices with their start and end apart: 5 -> 5, of which waited for: 2 -> 2; matrix products, arithmetic and copies ran while one was open for 18% -> 19% of each run, Pallas kernels for 0% -> 0%
where the time goes in v1:
time: 287 us; the launch traced here: 282 us
  matrix products  126 us (44%)
  waiting for transfers between devices  46.6 us (16%)
  local copies, waits for them, and re-layouts  43.1 us (15%)
  starting transfers between devices  26.1 us (9%)
  other arithmetic  21.3 us (7%)
  blocking collectives  18.4 us (6%)
    all_to_all x1, waiting for transfers between devices, local(): received = lax.all_to_all(jnp.stack(pieces), 'context', 0, 0)  24.9 us
    all_to_all x1, waiting for transfers between devices, local(): lax.all_to_all(products.reshape(context_size, local_channels, block_rows)...  21.8 us
    dot_general x2, matrix products, forward(): jnp.einsum('ckm,mj->ckj', turn_real, second_sin, precision=HIGHEST)  19.9 us
    all_gather x1, blocking collectives, local(): weights = lax.all_gather(short_filters, 'context', axis=2, tiled=True)  18.4 us
    dot_general x1, matrix products, causal_mix(): jnp.einsum('nk,ckm->cnm', first_cos[:half_rows, :], untwist_real, precisi...  17.8 us
    dot_general x1, matrix products, causal_mix(): jnp.einsum('nk,ckm->cnm', first_sin[:half_rows, :], untwist_imag, precisi...  17.4 us
    dot_general x2, matrix products, forward(): jnp.einsum('ckm,mj->ckj', turn_imag, second_cos, precision=HIGHEST)  17.2 us
    unnamed x47, local copies, waits for them, and re-layouts  17 us
  transfers between devices with their start and end apart: 5, of which 2 were waited for; matrix products, arithmetic and copies ran while one was open for 19% of the time, Pallas kernels for 0%

profile of v1, /device:TPU:13, one launch (start us, length us, event | category | flops | bytes accessed | tf_op | source)
XLA Modules:
  0.0 282.2 jit_solution(7059127035740623546)
XLA Ops:
  11.7 4.6 %all-to-all-start.1 = ((bf16[64,2,16,256]{3,2,0,1:T(8,128)(2,1)}), bf16[64,2,16,256]{3,2,0,1:T(8,128)(2,1)}, u32[]{:S(2)}, u32[]{:S(2)}) async-start(bf16[64,2,16,256]{3,2,0,1:T(8,128)(2,1)} %copy.141), calls=%async_computation.1 | async-start | bytes 2097152 | tf_op jit(solution)/shard_map/all_to_all | solution.py:86
  16.3 18.4 %all_gather.3 = f32[3,3,4096]{2,1,0:T(4,128)S(1)} all-gather(f32[3,3,256]{2,1,0:T(4,128)S(1)} %copy-done.12), channel_id=1, replica_groups=mesh['tensor'=2,'context'=16] {'context'}, dimensions={2}, use_global_device_ids=true | all-gather | bytes 156672 | tf_op jit(solution)/shard_map/all_gather | solution.py:91
  42.7 7.9 %fusion.29 = bf16[4096,128]{1,0:T(8,128)(2,1)} fusion(f32[4096,2]{1,0:T(8,128)S(1)} %get-tuple-element.12, f32[4096,128]{1,0:T(8,128)S(1)} %copy-done.8, f32[4096,2]{1,0:T(8,128)S(1)} %get-tuple-element.11, f32[4096,128]{1,0:T(8,128)S(1)} %copy-done.7, f32[4096]{0:T(1024)S(1)} %bitcast.202, f32[4096]{0:T(1024)S(1)} %bitcast.203, f32[4096]{0:T(1024)S(1)} %bitcast.204, ...), kind=kLoop, calls=%fused_computation.43 | loop fusion | flops 8388608 | bytes 5406720 | tf_op jit(solution)/shard_map/convert_element_type | solution.py:97
  50.6 6.5 %all-to-all-start = ((bf16[16,256,128]{2,1,0:T(8,128)(2,1)}), bf16[16,256,128]{2,1,0:T(8,128)(2,1)S(1)}, u32[]{:S(2)}, u32[]{:S(2)}) async-start(bf16[16,256,128]{2,1,0:T(8,128)(2,1)} %bitcast.15), calls=%async_computation | async-start | bytes 2097152 | tf_op jit(solution)/shard_map/all_to_all | solution.py:98
  60.3 21.8 %all-to-all-done = bf16[16,256,128]{2,1,0:T(8,128)(2,1)S(1)} async-done(((bf16[16,256,128]{2,1,0:T(8,128)(2,1)}), bf16[16,256,128]{2,1,0:T(8,128)(2,1)S(1)}, u32[]{:S(2)}, u32[]{:S(2)}) %all-to-all-start) | async-done | bytes 1048608 | tf_op jit(solution)/shard_map/all_to_all | solution.py:98
  82.1 5.1 %all-to-all-start.2 = ((bf16[128,1,16,256]{3,0,1,2:T(8,128)(2,1)}), bf16[128,1,16,256]{3,0,1,2:T(8,128)(2,1)S(1)}, u32[]{:S(2)}, u32[]{:S(2)}) async-start(bf16[128,1,16,256]{3,0,1,2:T(8,128)(2,1)} %copy.142), calls=%async_computation.2 | async-start | bytes 2097152 | tf_op jit(solution)/shard_map/all_to_all | solution.py:87
  96.6 6.4 %fusion.12 = f32[256,128,32]{1,2,0:T(8,128)S(1)} fusion(f32[256,128,32]{1,0,2:T(8,128)S(1)} %get-tuple-element.10), kind=kOutput, calls=%fused_computation.28 | convolution fusion | flops 402668544 | bytes 8388608 | tf_op jit(solution)/shard_map/ckm,mj->ckj/dot_general | solution.py:53
  102.9 9.5 %fusion.10 = f32[256,128,32]{1,2,0:T(8,128)} fusion(f32[256,128,32]{1,0,2:T(8,128)S(1)} %get-tuple-element.10), kind=kOutput, calls=%fused_computation.26 | convolution fusion | flops 402667520 | bytes 8388608 | tf_op jit(solution)/shard_map/ckm,mj->ckj/dot_general | solution.py:56
  112.4 8.9 %fusion.18 = f32[256,128,32]{1,2,0:T(8,128)} fusion(f32[256,128,32]{1,2,0:T(8,128)S(1)} %fusion.12, f32[256,128,32]{1,0,2:T(8,128)S(1)} %get-tuple-element.9), kind=kOutput, calls=%fused_computation.34 | convolution fusion | flops 403716096 | bytes 12582912 | tf_op jit(solution)/shard_map/ckm,mj->ckj/dot_general | solution.py:53
  123.0 5.6 %add_bitcast_fusion = (f32[256,128,32]{0,1,2:T(8,128)}, f32[256,128,32]{0,1,2:T(8,128)}) fusion(f32[128,256,32]{1,0,2:T(8,128)S(1)} %fusion.51, f32[128,32]{0,1:T(8,128)S(1)} %get-tuple-element.23, f32[128,32]{0,1:T(8,128)S(1)} %get-tuple-element.24, bf16[256,64,32]{0,2,1:T(8,128)(2,1)S(1)} %bitcast.192, f32[128,128]{0,1:T(8,128)S(1)} %fusion.81), kind=kOutput, calls=%fused_computation.24 | convolution fusion | flops 408944640 | bytes 13697024 | tf_op jit(solution)/shard_map/kn,cnm->ckm/dot_general | solution.py:49
  128.6 5.6 %copy.146 = f32[256,128,32]{1,2,0:T(8,128)} copy(f32[256,128,32]{0,1,2:T(8,128)} %get-tuple-element.8) | data formatting | bytes 8388608 | tf_op jit(solution)/shard_map/sub | solution.py:51
  134.2 8.0 %fusion.92 = f32[256,128,32]{1,2,0:T(8,128)} fusion(f32[256,128,32]{1,2,0:T(8,128)} %copy.146), kind=kOutput, calls=%fused_computation.144 | convolution fusion | flops 402668544 | bytes 8388608 | tf_op jit(solution)/shard_map/ckm,mj->ckj/dot_general | solution.py:56
  142.3 5.4 %fusion.103 = f32[256,128,32]{1,2,0:T(8,128)} fusion(f32[256,128,32]{1,2,0:T(8,128)S(1)} %copy-done.3), kind=kOutput, calls=%fused_computation.155 | convolution fusion | flops 402667520 | bytes 8388608 | tf_op jit(solution)/shard_map/ckm,mj->ckj/dot_general | solution.py:53
  147.7 5.5 %copy.147 = f32[256,128,32]{1,2,0:T(8,128)} copy(f32[256,128,32]{0,1,2:T(8,128)} %get-tuple-element.7) | data formatting | bytes 8388608 | tf_op jit(solution)/shard_map/add | solution.py:52
  153.1 7.7 %convolution_add_fusion = f32[256,128,32]{1,2,0:T(8,128)S(1)} fusion(f32[256,128,32]{1,2,0:T(8,128)} %fusion.92, f32[256,128,32]{1,2,0:T(8,128)} %copy.147), kind=kOutput, calls=%fused_computation.36 | convolution fusion | flops 403716096 | bytes 12582912 | tf_op jit(solution)/shard_map/ckm,mj->ckj/dot_general | solution.py:56
  160.9 5.3 %convolution_subtract_fusion = f32[256,128,32]{1,2,0:T(8,128)} fusion(f32[256,128,32]{1,2,0:T(8,128)S(1)} %copy-done.5, f32[256,128,32]{1,2,0:T(8,128)S(1)} %copy-done.2), kind=kOutput, calls=%fused_computation.37 | convolution fusion | flops 403717120 | bytes 12582912 | tf_op jit(solution)/shard_map/ckm,mj->ckj/dot_general | solution.py:53
  166.2 11.8 %multiply_subtract_fusion = (f32[256,128,32]{1,2,0:T(8,128)S(1)}, f32[256,128,32]{1,2,0:T(8,128)S(1)}) fusion(f32[256,128,32]{1,2,0:T(8,128)S(1)} %convolution_add_fusion, f32[256,128,32]{1,2,0:T(8,128)S(1)} %copy-done.4, f32[256,128,32]{1,2,0:T(8,128)} %convolution_subtract_fusion, f32[256,128,32]{1,2,0:T(8,128)} %fusion.10, f32[256,128,32]{1,0,2:T(8,128)S(1)} %copy-done.1), kind=kOutput, calls=%fused_computation.23 | convolution fusion | flops 410008576 | bytes 29360128 | tf_op jit(solution)/shard_map/ckm,mj->ckj/dot_general | solution.py:56
  186.1 4.1 %fusion.88 = f32[256,128,32]{1,2,0:T(8,128)S(1)} fusion(f32[256,128,32]{1,2,0:T(8,128)S(1)} %get-tuple-element.5), kind=kOutput, calls=%fused_computation.140 | convolution fusion | flops 402668544 | bytes 8388608 | tf_op jit(solution)/shard_map/ckm,mj->ckj/dot_general | solution.py:68
  190.2 4.2 %fusion.99 = f32[256,128,32]{1,2,0:T(8,128)S(1)} fusion(f32[256,128,32]{1,2,0:T(8,128)S(1)} %get-tuple-element.5), kind=kOutput, calls=%fused_computation.151 | convolution fusion | flops 402667520 | bytes 8388608 | tf_op jit(solution)/shard_map/ckm,mj->ckj/dot_general | solution.py:65
  194.4 17.4 %fusion.2 = f32[256,32,64]{0,2,1:T(8,128)S(1)} fusion(f32[128,32]{0,1:T(8,128)S(1)} %get-tuple-element.23, f32[128,32]{0,1:T(8,128)S(1)} %get-tuple-element.24, f32[256,128,32]{1,2,0:T(8,128)S(1)} %fusion.90, f32[256,128,32]{1,2,0:T(8,128)S(1)} %fusion.99, f32[256,128,32]{1,2,0:T(8,128)S(1)} %fusion.88, f32[256,128,32]{1,2,0:T(8,128)S(1)} %fusion.97, ...), kind=kOutput, calls=%fused_computation.14 | convolution fusion | flops 810549248 | bytes 18972672 | tf_op jit(solution)/shard_map/nk,ckm->cnm/dot_general | solution.py:75
  211.9 17.8 %multiply_bitcast_fusion = f32[256,64,32]{0,1,2:T(8,128)S(1)} fusion(f32[256,32,64]{0,2,1:T(8,128)S(1)} %fusion.2, f32[128,32]{0,1:T(8,128)S(1)} %get-tuple-element.23, f32[128,32]{0,1:T(8,128)S(1)} %get-tuple-element.24, f32[256,128,32]{1,2,0:T(8,128)S(1)} %fusion.90, f32[256,128,32]{1,2,0:T(8,128)S(1)} %fusion.99, f32[256,128,32]{1,2,0:T(8,128)S(1)} %fusion.88, ...), kind=kOutput, calls=%fused_computation.66 | convolution fusion | flops 811597824 | bytes 21069824 | tf_op jit(solution)/shard_map/nk,ckm->cnm/dot_general | solution.py:73
  241.8 6.0 %all-to-all-start.3 = ((bf16[16,1,256,128]{2,3,1,0:T(8,128)(2,1)}), bf16[16,1,256,128]{2,3,1,0:T(8,128)(2,1)}, u32[]{:S(2)}, u32[]{:S(2)}) async-start(bf16[16,1,256,128]{2,3,1,0:T(8,128)(2,1)} %fusion.62), calls=%async_computation.3 | async-start | bytes 2097152 | tf_op jit(solution)/shard_map/all_to_all | solution.py:110
  248.0 24.9 %all-to-all-done.3 = bf16[16,1,256,128]{2,3,1,0:T(8,128)(2,1)} async-done(((bf16[16,1,256,128]{2,3,1,0:T(8,128)(2,1)}), bf16[16,1,256,128]{2,3,1,0:T(8,128)(2,1)}, u32[]{:S(2)}, u32[]{:S(2)}) %all-to-all-start.3) | async-done | bytes 1048608 | tf_op jit(solution)/shard_map/all_to_all | solution.py:110
  275.5 6.5 %fusion.39 = bf16[4096,128]{1,0:T(8,128)(2,1)} fusion(f32[4096,2]{1,0:T(8,128)} %get-tuple-element.13, f32[4096,128]{1,0:T(8,128)S(1)} %convert_element_type.118, f32[16,1,256,128]{3,2,0,1:T(8,128)} %copy.160, f32[4096]{0:T(1024)S(1)} %bitcast.200, f32[4096]{0:T(1024)S(1)} %bitcast.201, f32[4096]{0:T(1024)S(1)} %bitcast.199), kind=kLoop, calls=%fused_computation.53 | loop fusion | flops 4718592 | bytes 5324800 | tf_op jit(solution)/shard_map/convert_element_type | solution.py:113
  (77 shorter events, 56.6 us)
Async XLA Ops:
  0.0 3.1 %copy-start.10 = (bf16[4096,128]{1,0:T(8,128)(2,1)S(1)}, bf16[4096,128]{1,0:T(8,128)(2,1)}, u32[]{:S(2)}) copy-start(bf16[4096,128]{1,0:T(8,128)(2,1)} %param.8) | copy-start | bytes 3145732
  4.4 11.9 %copy-start.12 = (f32[3,3,256]{2,1,0:T(4,128)S(1)}, f32[3,3,256]{2,1,0:T(4,128)}, u32[]{:S(2)}) copy-start(f32[3,3,256]{2,1,0:T(4,128)} %param.10) | copy-start | bytes 27652
  5.3 29.5 %copy-start.9 = (bf16[4096,128]{1,0:T(8,128)(2,1)S(1)}, bf16[4096,128]{1,0:T(8,128)(2,1)}, u32[]{:S(2)}) copy-start(bf16[4096,128]{1,0:T(8,128)(2,1)} %param.7) | copy-start | bytes 3145732
  5.3 32.4 %collective-permute-start = (bf16[3,4096,2]{1,2,0:T(2,128)(2,1)S(1)}, bf16[3,4096,2]{1,2,0:T(2,128)(2,1)S(1)}, u32[]{:S(2)}, u32[]{:S(2)}) collective-permute-start(bf16[3,4096,2]{1,2,0:T(2,128)(2,1)S(1)} %pad_maximum_fusion.3), channel_id=1, source_target_pairs={{0,1},{1,2},{2,3},{3,4},{4,5},{5,6},{6,7},{7,8},{8,9},{9,10},{10,1... | collective-permute-start | bytes 147464 | tf_op jit(solution)/shard_map/ppermute | solution.py:15
  11.7 38.9 %all-to-all-start.1 = ((bf16[64,2,16,256]{3,2,0,1:T(8,128)(2,1)}), bf16[64,2,16,256]{3,2,0,1:T(8,128)(2,1)}, u32[]{:S(2)}, u32[]{:S(2)}) async-start(bf16[64,2,16,256]{3,2,0,1:T(8,128)(2,1)} %copy.141), calls=%async_computation.1 | async-start | bytes 2097152 | tf_op jit(solution)/shard_map/all_to_all | solution.py:86
  39.7 2.1 copy-start.7
  39.7 3.0 %copy-start.8 = (f32[4096,128]{1,0:T(8,128)S(1)}, f32[4096,128]{1,0:T(8,128)}, u32[]{:S(2)}) copy-start(f32[4096,128]{1,0:T(8,128)} %convert_element_type.121) | copy-start | bytes 6291460
  50.6 31.5 %all-to-all-start = ((bf16[16,256,128]{2,1,0:T(8,128)(2,1)}), bf16[16,256,128]{2,1,0:T(8,128)(2,1)S(1)}, u32[]{:S(2)}, u32[]{:S(2)}) async-start(bf16[16,256,128]{2,1,0:T(8,128)(2,1)} %bitcast.15), calls=%async_computation | async-start | bytes 2097152 | tf_op jit(solution)/shard_map/all_to_all | solution.py:98
  82.1 39.3 %all-to-all-start.2 = ((bf16[128,1,16,256]{3,0,1,2:T(8,128)(2,1)}), bf16[128,1,16,256]{3,0,1,2:T(8,128)(2,1)S(1)}, u32[]{:S(2)}, u32[]{:S(2)}) async-start(bf16[128,1,16,256]{3,0,1,2:T(8,128)(2,1)} %copy.142), calls=%async_computation.2 | async-start | bytes 2097152 | tf_op jit(solution)/shard_map/all_to_all | solution.py:87
  96.6 15.9 %copy-start = (f32[256,128,32]{1,0,2:T(8,128)}, f32[256,128,32]{1,0,2:T(8,128)S(1)}, u32[]{:S(2)}) copy-start(f32[256,128,32]{1,0,2:T(8,128)S(1)} %get-tuple-element.9) | copy-start | bytes 12582916
  134.2 8.1 %copy-start.3 = (f32[256,128,32]{1,2,0:T(8,128)S(1)}, f32[256,128,32]{1,2,0:T(8,128)}, u32[]{:S(2)}) copy-start(f32[256,128,32]{1,2,0:T(8,128)} %copy.146) | copy-start | bytes 12582916
  153.1 7.7 %copy-start.2 = (f32[256,128,32]{1,2,0:T(8,128)S(1)}, f32[256,128,32]{1,2,0:T(8,128)}, u32[]{:S(2)}) copy-start(f32[256,128,32]{1,2,0:T(8,128)} %copy.147) | copy-start | bytes 12582916
  153.1 7.7 %copy-start.5 = (f32[256,128,32]{1,2,0:T(8,128)S(1)}, f32[256,128,32]{1,2,0:T(8,128)}, u32[]{:S(2)}) copy-start(f32[256,128,32]{1,2,0:T(8,128)} %fusion.103) | copy-start | bytes 12582916
  160.9 5.3 %copy-start.1 = (f32[256,128,32]{1,0,2:T(8,128)S(1)}, f32[256,128,32]{1,0,2:T(8,128)}, u32[]{:S(2)}) copy-start(f32[256,128,32]{1,0,2:T(8,128)} %copy-done) | copy-start | bytes 12582916
  160.9 5.3 %copy-start.4 = (f32[256,128,32]{1,2,0:T(8,128)S(1)}, f32[256,128,32]{1,2,0:T(8,128)}, u32[]{:S(2)}) copy-start(f32[256,128,32]{1,2,0:T(8,128)} %fusion.18) | copy-start | bytes 12582916
  229.7 1.6 copy-start.6
  229.7 1.6 copy-start.13
  231.3 16.5 %copy-start.11 = (bf16[4096,128]{1,0:T(8,128)(2,1)S(1)}, bf16[4096,128]{1,0:T(8,128)(2,1)}, u32[]{:S(2)}) copy-start(bf16[4096,128]{1,0:T(8,128)(2,1)} %param.6) | copy-start | bytes 3145732
  241.8 31.0 %all-to-all-start.3 = ((bf16[16,1,256,128]{2,3,1,0:T(8,128)(2,1)}), bf16[16,1,256,128]{2,3,1,0:T(8,128)(2,1)}, u32[]{:S(2)}, u32[]{:S(2)}) async-start(bf16[16,1,256,128]{2,3,1,0:T(8,128)(2,1)} %fusion.62), calls=%async_computation.3 | async-start | bytes 2097152 | tf_op jit(solution)/shard_map/all_to_all | solution.py:110
